TPU v7x, 256 devices: a whole 4x4x8 slice. The times are simulated.
256 devices in a mesh: gy: 8 (over z), gx: 32 (over y, x, core).
Axes of the slice: x: 4, y: 4, z: 8, core: 2. Of those that a mesh axis runs over, the one named last changes fastest.
Arguments:
- positions: float32 [3, 32, 65536], P(None, 'gx', 'gy'), may hold values from -6 to 6
- velocities: float32 [3, 32, 65536], P(None, 'gx', 'gy'), may hold values from -6 to 6
- radius: float32 [32, 65536], P('gx', 'gy'), may hold values from 0.6 to 1
- sphere_cell: int32 [32, 65536], P('gx', 'gy'), may hold values from -1 to 16383, as said below
- pair_route: int32 [32, 512, 1], P('gx', 'gy'), may hold values from 0 to 30; in each aligned block of 64 rows (0 to 63, 64 to 127, ..., all dimensions but the last counted through in order) at most 4 rows name the same one
- pair_mine: int32 [32, 512], P('gx', 'gy'), may hold values from 0 to 63
- pair_theirs: int32 [32, 512], P('gx', 'gy'), may hold values from 0 to 63
- brick_owner: int32 [32, 8], P('gx'), may hold values from 0 to 7, each once within a row
- fluid_velocity: float32 [3, 32, 16384], P(None, 'gx', 'gy'), may hold values from -6 to 6
- pressure_grad: float32 [3, 32, 16384], P(None, 'gx', 'gy'), may hold values from -6 to 6
Outputs:
- new_velocity: float32 [3, 32, 65536], P(None, 'gx', 'gy')
- drag_source: float32 [3, 32, 16384], P(None, 'gx', 'gy')
Inputs may be any that keep to these rules, and one draw needn't show every extreme that they name: `pair_route`: the pairs of one device name one offset at most 4 times, a bound that some block reaches. `sphere_cell`: in every block of 128 slots the live slots come first and are half of the block or more; every device has a full block.
All inputs are finite; a program needn't handle non-finite values.
Results may differ from a plain program's by a relative error of at most 0.0003.
Values sent between devices are 32-bit elements; how exact they have to be, the bound alone decides.
No kernel may reach another device: no remote copies, remote signals or barrier semaphores. Data moves between devices by JAX's collectives and lax.ppermute only.
A program may use at most 128 MiB of HBM per device.

v0:
```python
import math

import jax
import jax.numpy as jnp
from jax import lax
from jax.sharding import PartitionSpec as P

stiffness = 0.05
damping = 0.02
drag_coeff = 0.5
time_step = 0.2


def contact(left_state, right_state):
    offset = left_state[:, 0:3, :, None] - right_state[:, 0:3, None, :]
    dist_sq = (
        offset[:, 0] * offset[:, 0] + offset[:, 1] * offset[:, 1] + offset[:, 2] * offset[:, 2]
    )
    radius_sum = left_state[:, 6, :, None] + right_state[:, 6, None, :]
    weight = jnp.exp(-dist_sq / (2.0 * radius_sum * radius_sum)) * (
        left_state[:, 7, :, None] * right_state[:, 7, None, :]
    )
    relative = left_state[:, 3:6, :, None] - right_state[:, 3:6, None, :]
    pulling = weight[:, None] * (stiffness * offset - damping * relative)
    return (jnp.sum(pulling, axis=3), -jnp.sum(pulling, axis=2))


def contact_pair(pair_in):
    return contact(pair_in[0], pair_in[1])


def grouped(left_all, right_all):
    count_all = left_all.shape[0]
    width = left_all.shape[2]
    group_size = math.gcd(count_all, 8)
    shaped = (
        left_all.reshape(count_all // group_size, group_size, 8, width),
        right_all.reshape(count_all // group_size, group_size, 8, width),
    )
    on_left, on_right = lax.map(contact_pair, shaped)
    return (on_left.reshape(count_all, 3, width), on_right.reshape(count_all, 3, width))


def on_device(
    positions,
    velocities,
    radius,
    sphere_cell,
    pair_route,
    pair_mine,
    pair_theirs,
    brick_owner,
    fluid_velocity,
    pressure_grad,
):
    width = 128
    sphere_total = positions.shape[2]
    blocks = sphere_total // width
    alive_mask = (sphere_cell[0] >= 0).astype(jnp.float32)
    states = jnp.concatenate(
        [positions[:, 0], velocities[:, 0], radius[0][None], alive_mask[None]], axis=0
    )
    states = states.reshape(8, blocks, width).transpose(1, 0, 2)
    gy_count = lax.axis_size("gy")
    cells_dev = fluid_velocity.shape[2]
    column_u, column_p = (
        lax.all_gather(fluid_velocity, "gy", axis=2, tiled=True),
        lax.all_gather(pressure_grad, "gy", axis=2, tiled=True),
    )
    gx_count = lax.axis_size("gx")
    my_index = lax.axis_index("gx")
    pair_total = pair_route.shape[1]
    capacity = max(2, 2 * pair_total // gx_count)
    slot_total = gx_count * capacity
    target = (my_index + 1 + pair_route[0, :, 0]) % gx_count
    onehot_target = (target[:, None] == jnp.arange(gx_count, dtype=jnp.int32)[None, :]).astype(
        jnp.int32
    )
    order_in = jnp.sum(jnp.cumsum(onehot_target, axis=0) * onehot_target, axis=1) - 1
    slot_index = target * capacity + order_in
    wanted = jnp.full((slot_total,), -1, jnp.int32).at[slot_index].set(pair_theirs[0])
    owned_block = jnp.zeros((slot_total,), jnp.int32).at[slot_index].set(pair_mine[0])
    asked = lax.all_to_all(
        wanted.reshape(gx_count, capacity), "gx", split_axis=0, concat_axis=0, tiled=True
    )
    valid_ask = (asked >= 0).astype(jnp.float32)
    served = states[jnp.clip(asked, 0, blocks - 1)] * valid_ask[:, :, None, None]
    partner = lax.all_to_all(served, "gx", split_axis=0, concat_axis=0, tiled=True)
    own_slots = states[owned_block].reshape(gx_count, capacity, 8, width)
    beside = jnp.concatenate([states[1:], jnp.zeros_like(states[:1])], axis=0)
    self_force, unused_self = grouped(states, states)
    near_force, back_force = grouped(states, beside)
    local_force = (
        self_force
        + near_force
        + jnp.concatenate([jnp.zeros_like(back_force[:1]), back_force[:-1]], axis=0)
    )
    on_owner, on_partner = grouped(
        own_slots.reshape(slot_total, 8, width), partner.reshape(slot_total, 8, width)
    )
    returned = lax.all_to_all(
        on_partner.reshape(gx_count, capacity, 3, width),
        "gx",
        split_axis=0,
        concat_axis=0,
        tiled=True,
    )
    block_ids = jnp.arange(blocks, dtype=jnp.int32)[:, None]
    owner_hot = (owned_block[None, :] == block_ids).astype(jnp.float32)
    served_hot = (asked.reshape(-1)[None, :] == block_ids).astype(jnp.float32)
    remote_force = jnp.dot(
        owner_hot,
        on_owner.reshape(slot_total, 3 * width),
        precision=lax.Precision.HIGHEST,
        preferred_element_type=jnp.float32,
    )
    remote_force = remote_force + jnp.dot(
        served_hot,
        returned.reshape(slot_total, 3 * width),
        precision=lax.Precision.HIGHEST,
        preferred_element_type=jnp.float32,
    )
    total_force = local_force + remote_force.reshape(blocks, 3, width)
    contact_force = total_force.transpose(1, 0, 2).reshape(3, sphere_total)
    cell_here = sphere_cell[0]
    block_of = cell_here // cells_dev
    within = cell_here % cells_dev
    owner_of = jnp.sum(
        jnp.where(
            block_of[:, None] == jnp.arange(gy_count, dtype=jnp.int32)[None, :],
            brick_owner[0][None, :],
            0,
        ),
        axis=1,
    )
    storage = jnp.where(cell_here >= 0, owner_of * cells_dev + within, 0)
    fluid_at = jnp.take(column_u[:, 0], storage, axis=1)
    grad_at = jnp.take(column_p[:, 0], storage, axis=1)
    speed = velocities[:, 0]
    radii = radius[0]
    sphere_cube = radii * radii * radii
    drag_force = alive_mask * drag_coeff * radii * (fluid_at - speed)
    fluid_force = drag_force - alive_mask * sphere_cube * grad_at
    new_velocity = speed + time_step * (contact_force + fluid_force) / sphere_cube
    deposit = jax.ops.segment_sum(-drag_force.T, storage, num_segments=gy_count * cells_dev)
    drag_source = lax.psum_scatter(
        deposit.T.reshape(3, 1, gy_count * cells_dev), "gy", scatter_dimension=2, tiled=True
    )
    return (new_velocity.reshape(3, 1, sphere_total), drag_source)


def solution(mesh):
    placed = (
        P(None, "gx", "gy"),
        P(None, "gx", "gy"),
        P("gx", "gy"),
        P("gx", "gy"),
        P("gx", "gy", None),
        P("gx", "gy"),
        P("gx", "gy"),
        P("gx", None),
        P(None, "gx", "gy"),
        P(None, "gx", "gy"),
    )
    return jax.shard_map(
        on_device,
        mesh=mesh,
        in_specs=placed,
        out_specs=(P(None, "gx", "gy"), P(None, "gx", "gy")),
        check_vma=False,
    )
```

profile of v0, /device:TPU:1, one launch (start us, length us, event | category | flops | bytes accessed | tf_op | source)
XLA Modules:
  0.0 487.1 jit_solution(10274838143730980073)
XLA Ops:
  10.5 8.6 %all-to-all-start = ((s32[32,1,4]{2,1,0:T(1,128)}), s32[32,1,4]{2,1,0:T(1,128)S(1)}, u32[]{:S(2)}, u32[]{:S(2)}) async-start(s32[32,1,4]{2,1,0:T(1,128)} %bitcast.43), calls=%async_computation | async-start | bytes 32768 | tf_op jit(solution)/shard_map/all_to_all | solution.py:83
  22.7 86.4 %all_gather.6 = f32[3,1,16384]{0,2,1:T(8,128)} all-gather(f32[3,1,2048]{0,2,1:T(8,128)S(1)} %copy.106), channel_id=1, replica_groups=mesh['gy'=8,'gx'=32] {'gy'}, dimensions={2}, use_global_device_ids=true | all-gather | bytes 221184 | tf_op jit(solution)/shard_map/all_gather | solution.py:67
  109.2 2.7 copy.92
  111.9 31.1 %gather_fusion.2 = f32[8192,3]{1,0:T(8,128)} fusion(f32[3,16384]{0,1:T(8,128)} %bitcast.186, s32[8192]{0:T(1024)S(1)} %broadcast_clamp_fusion), kind=kCustom, calls=%fused_computation.clone | custom fusion | bytes 229376 | tf_op jit(solution)/shard_map/jit(_take)/gather | solution.py:137
  143.0 56.0 %scatter_custom_fusion.2 = f32[16384,3]{1,0:T(8,128)} fusion(s32[8192]{0:T(1024)S(1)} %bitcast.218, f32[]{:T(128)} %constant.139.clone.1, f32[3,1,8192]{0,2,1:T(8,128)} %copy.92, f32[8192,3]{1,0:T(8,128)} %gather_fusion.2, f32[]{:T(128)} %constant.137.clone.2, f32[8192]{0:T(1024)S(1)} %bitcast.209, pred[8192]{0:T(1024)(128)(4,1)S(1)} %get-tuple-element.135), kind=kCustom, calls=%fused_computation.60 | custom fusion | flops 122880 | bytes 434184 | tf_op jit(solution)/shard_map/scatter-add | solution.py:145
  200.4 20.6 %while.36 = (s32[]{:T(128)}, f32[8,8,3,128]{3,2,1,0:T(4,128)S(1)}, f32[8,8,3,128]{3,2,1,0:T(4,128)S(1)}, f32[8,8,8,128]{3,2,1,0:T(8,128)S(1)}, f32[8,8,8,128]{3,2,1,0:T(8,128)S(1)}, /*index=5*/s32[]{:T(128)}) while((s32[]{:T(128)}, f32[8,8,3,128]{3,2,1,0:T(4,128)S(1)}, f32[8,8,3,128]{3,2,1,0:T(4,128)S(1)}, f32[8,8,8,128]{3,2,1,0:T(8,128)S(1)}, ...), condition=%wide.region_6.7_spmd, body=%wide.region_3.6_spmd.sunk | while | flops 5108738 | bytes 4636753 | solution.py:40
  201.4 1.6 fusion.98
  203.9 1.6 fusion.98
  206.5 1.6 fusion.98
  209.1 1.6 fusion.98
  211.7 1.6 fusion.98
  214.2 1.6 fusion.98
  216.8 1.6 fusion.98
  223.2 8.6 %all-to-all-start.1 = ((f32[32,4,8,128]{3,2,1,0:T(8,128)}), f32[32,4,8,128]{3,2,1,0:T(8,128)S(1)}, u32[]{:S(2)}, u32[]{:S(2)}) async-start(f32[32,4,8,128]{3,2,1,0:T(8,128)} %broadcast_multiply_fusion), calls=%async_computation.1 | async-start | bytes 1048576 | tf_op jit(solution)/shard_map/all_to_all | solution.py:88
  231.8 19.1 %while.35 = (s32[]{:T(128)}, f32[8,8,3,128]{3,2,1,0:T(4,128)S(1)}, f32[8,8,8,128]{3,2,1,0:T(8,128)S(1)}, s32[]{:T(128)}) while((s32[]{:T(128)}, f32[8,8,3,128]{3,2,1,0:T(4,128)S(1)}, f32[8,8,8,128]{3,2,1,0:T(8,128)S(1)}, s32[]{:T(128)}) %tuple.115), condition=%wide.region_2.3_spmd, body=%wide.region_0.2_spmd.sunk | while | flops 4715522 | bytes 4423741 | solution.py:40
  253.1 118.4 %all_gather.7 = f32[3,1,16384]{0,2,1:T(8,128)} all-gather(f32[3,1,2048]{0,2,1:T(8,128)S(1)} %copy.107), channel_id=1, replica_groups=mesh['gy'=8,'gx'=32] {'gy'}, dimensions={2}, use_global_device_ids=true | all-gather | bytes 221184 | tf_op jit(solution)/shard_map/all_gather | solution.py:68
  371.5 31.1 %gather_fusion.3 = f32[8192,3]{1,0:T(8,128)} fusion(f32[3,16384]{0,1:T(8,128)} %bitcast.187, s32[8192]{0:T(1024)S(1)} %broadcast_clamp_fusion), kind=kCustom, calls=%fused_computation.1.clone | custom fusion | bytes 229376 | tf_op jit(solution)/shard_map/jit(_take)/gather | solution.py:138
  404.0 2.2 copy.109
  406.2 41.1 %while.37 = (s32[]{:T(128)}, f32[16,8,3,128]{3,2,1,0:T(4,128)S(1)}, f32[16,8,3,128]{3,2,1,0:T(4,128)S(1)}, f32[16,8,8,128]{3,2,1,0:T(8,128)S(1)}, f32[16,8,8,128]{3,2,1,0:T(8,128)S(1)}, /*index=5*/s32[]{:T(128)}) while((s32[]{:T(128)}, f32[16,8,3,128]{3,2,1,0:T(4,128)S(1)}, f32[16,8,3,128]{3,2,1,0:T(4,128)S(1)}, ...), condition=%wide.region_14.15_spmd, body=%wide.region_11.14_spmd.sunk | while | flops 5108738 | bytes 4636753 | solution.py:40
  448.0 7.4 %all-to-all-start.2 = ((f32[32,4,3,128]{3,1,2,0:T(4,128)}), f32[32,4,3,128]{3,1,2,0:T(4,128)S(1)}, u32[]{:S(2)}, u32[]{:S(2)}) async-start(f32[32,4,3,128]{3,1,2,0:T(4,128)} %copy.103), calls=%async_computation.2 | async-start | bytes 393216 | tf_op jit(solution)/shard_map/all_to_all | solution.py:101
  455.7 8.0 %all-to-all-done.2 = f32[32,4,3,128]{3,1,2,0:T(4,128)S(1)} async-done(((f32[32,4,3,128]{3,1,2,0:T(4,128)}), f32[32,4,3,128]{3,1,2,0:T(4,128)S(1)}, u32[]{:S(2)}, u32[]{:S(2)}) %all-to-all-start.2) | async-done | bytes 196640 | tf_op jit(solution)/shard_map/all_to_all | solution.py:101
  464.1 2.6 copy.105
  466.7 10.1 %fusion.32 = f32[3,1,8192]{0,2,1:T(8,128)} fusion(f32[3,64,128]{0,2,1:T(8,128)} %copy.105, f32[3,1,8192]{0,2,1:T(8,128)} %copy.92, f32[8192,3]{1,0:T(8,128)} %gather_fusion.3, f32[8192,3]{1,0:T(8,128)} %gather_fusion.2, f32[8192]{0:T(1024)S(1)} %bitcast.215, f32[8192]{0:T(1024)S(1)} %bitcast.214, f32[8192]{0:T(1024)S(1)} %bitcast.210, ...), kind=kLoop, calls=%fused_computation.68 | loop fusion | flops 245760 | bytes 598016 | tf_op jit(solution)/shard_map/reshape | solution.py:149
  476.8 3.5 copy.108
  (356 shorter events, 82.6 us)
Async XLA Ops:
  10.5 210.5 %all-to-all-start = ((s32[32,1,4]{2,1,0:T(1,128)}), s32[32,1,4]{2,1,0:T(1,128)S(1)}, u32[]{:S(2)}, u32[]{:S(2)}) async-start(s32[32,1,4]{2,1,0:T(1,128)} %bitcast.43), calls=%async_computation | async-start | bytes 32768 | tf_op jit(solution)/shard_map/all_to_all | solution.py:83
  19.1 384.9 %reduce-scatter.2.cloned.1.call-start = ((), (), s32[]{:S(2)}) async-start(), calls=%async_computation.4 | async-start | bytes 9437184 | tf_op jit(solution)/shard_map/reduce_scatter | solution.py:146
  22.6 86.4 %copy-start = (s32[1,8192]{1,0:T(1,128)S(1)}, s32[1,8192]{1,0:T(1,128)}, u32[]{:S(2)}) copy-start(s32[1,8192]{1,0:T(1,128)} %param.21) | copy-start | bytes 98308
  22.7 86.4 %copy-start.2 = (f32[1,8192]{1,0:T(1,128)S(1)}, f32[1,8192]{1,0:T(1,128)}, u32[]{:S(2)}) copy-start(f32[1,8192]{1,0:T(1,128)} %param.20) | copy-start | bytes 98308
  22.7 86.5 %copy-start.1 = (f32[3,1,8192]{2,1,0:T(1,128)S(1)}, f32[3,1,8192]{2,1,0:T(1,128)}, u32[]{:S(2)}) copy-start(f32[3,1,8192]{2,1,0:T(1,128)} %param.19) | copy-start | bytes 294916
  199.0 0.9 copy-start.3
  223.2 183.0 %all-to-all-start.1 = ((f32[32,4,8,128]{3,2,1,0:T(8,128)}), f32[32,4,8,128]{3,2,1,0:T(8,128)S(1)}, u32[]{:S(2)}, u32[]{:S(2)}) async-start(f32[32,4,8,128]{3,2,1,0:T(8,128)} %broadcast_multiply_fusion), calls=%async_computation.1 | async-start | bytes 1048576 | tf_op jit(solution)/shard_map/all_to_all | solution.py:88
  231.8 20.9 %copy-start.4 = (f32[3,1,2048]{2,1,0:T(1,128)S(1)}, f32[3,1,2048]{2,1,0:T(1,128)}, u32[]{:S(2)}) copy-start(f32[3,1,2048]{2,1,0:T(1,128)} %param.27) | copy-start | bytes 73732
  448.0 15.7 %all-to-all-start.2 = ((f32[32,4,3,128]{3,1,2,0:T(4,128)}), f32[32,4,3,128]{3,1,2,0:T(4,128)S(1)}, u32[]{:S(2)}, u32[]{:S(2)}) async-start(f32[32,4,3,128]{3,1,2,0:T(4,128)} %copy.103), calls=%async_computation.2 | async-start | bytes 393216 | tf_op jit(solution)/shard_map/all_to_all | solution.py:101
Sparse Core Ops, SparseCore 0:
  199.2 129.3 reduce-scatter.1
where the time goes:
time: 488 us; the launch traced here: 487 us
  blocking collectives  205 us (42%)
  other arithmetic  149 us (31%)
  local copies, waits for them, and re-layouts  83.3 us (17%)
  starting transfers between devices  24.6 us (5%)
  between operations  14.4 us (3%)
  waiting for transfers between devices  8.06 us (2%)
    all_gather x1, blocking collectives, on_device(): lax.all_gather(pressure_grad, 'gy', axis=2, tiled=True)  118 us
    all_gather x1, blocking collectives, on_device(): lax.all_gather(fluid_velocity, 'gy', axis=2, tiled=True)  86.4 us
    scatter-add x1, other arithmetic, on_device(): jax.ops.segment_sum(-drag_force.T, storage, num_segments=gy_count * cells...  56 us
    reduce_sum x32, other arithmetic, contact(): return (jnp.sum(pulling, axis=3), -jnp.sum(pulling, axis=2))  49.8 us
    gather x1, local copies, waits for them, and re-layouts, on_device(): grad_at = jnp.take(column_p[:, 0], storage, axis=1)  31.1 us
    gather x1, local copies, waits for them, and re-layouts, on_device(): fluid_at = jnp.take(column_u[:, 0], storage, axis=1)  31.1 us
    sub x32, other arithmetic, contact(): offset = left_state[:, 0:3, :, None] - right_state[:, 0:3, None, :]  14.9 us
    mul x32, other arithmetic, contact(): pulling = weight[:, None] * (stiffness * offset - damping * relative)  11.5 us
  transfers between devices with their start and end apart: 4, of which 1 were waited for; matrix products, arithmetic and copies ran while one was open for 35% of the time, Pallas kernels for 0%

commit v1 on v0

v1 whole, which is shorter than its diff:
```python
import functools

import jax
import jax.numpy as jnp
from jax import lax
from jax.experimental import pallas as pl
from jax.experimental.pallas import tpu as pltpu
from jax.sharding import PartitionSpec as P


stiffness = 0.05
damping = 0.02
drag_coeff = 0.5
time_step = 0.2

LANES = 128
CAP = 4
UNROLL = 4
CHUNK = 4
WIDE = 2
SPLIT = 256
HALF_LOG2E = 0.7213475204444817
F32 = jnp.float32
BF16 = jnp.bfloat16

VMEM_SPEC = pl.BlockSpec(memory_space=pltpu.VMEM)
RAW_SPEC = pl.BlockSpec(memory_space=pl.ANY)
SMEM_SPEC = pl.BlockSpec(memory_space=pltpu.SMEM)


def pieces(value, count):
    found = []
    rest = value
    for step in range(count):
        part = rest.astype(BF16).astype(F32)
        found.append(part)
        if step + 1 < count:
            rest = rest - part
    return found


def row_ids(shape):
    return lax.broadcasted_iota(jnp.int32, shape, 0)


def prep_kernel(gx_count, route, mine, theirs, pos, vel, rad, cell, push, slots, state, used):
    me = lax.axis_index("gx")
    blocks = rad.shape[0]
    for c in range(3):
        state[0:blocks, c, :] = stiffness * pos[c] - damping * vel[c]
        state[0:blocks, 4 + c, :] = pos[c]
    state[0:blocks, 3, :] = (cell[...] >= 0).astype(F32)
    state[0:blocks, 7, :] = rad[...]
    state[blocks] = jnp.zeros((8, LANES), F32)
    push[...] = jnp.zeros(push.shape, F32)

    def clear(t, carry):
        used[t] = 0
        return carry

    lax.fori_loop(0, gx_count, clear, 0, unroll=8)
    tag = (row_ids((8, LANES)) == 3) & (lax.broadcasted_iota(jnp.int32, (8, LANES), 1) == 0)

    def place(p, carry):
        dest = lax.rem(me + 1 + route[p], gx_count)
        order = used[dest]
        used[dest] = order + 1
        slot = dest * CAP + order
        slots[p] = slot
        label = (theirs[p] + 1).astype(F32)
        push[slot] = jnp.where(tag, label, state[mine[p]])
        return carry

    lax.fori_loop(0, route.shape[0], place, 0, unroll=4)


def split_state(tile):
    rows = row_ids(tile.shape)
    scaled = jnp.where(rows < 4, 0.0, jnp.where(rows < 7, tile * (HALF_LOG2E**0.5), tile))
    square = scaled * scaled
    dist = jnp.sum(jnp.where(rows < 7, square, 0.0), axis=0, keepdims=True)
    size = jnp.sum(jnp.where(rows == 7, square, 0.0), axis=0, keepdims=True)
    return rows, scaled, dist, size


def norm_tile(rows, at, value, other):
    first, second, third = pieces(value, 3)
    inner = jnp.where(rows == at, first, jnp.where(rows == at + 1, second, third))
    here = (rows >= at) & (rows < at + 3)
    return jnp.where(here, inner, jnp.where(rows < 6, other, 0.0))


def right_features(tile):
    rows, scaled, dist, size = split_state(tile)
    high, mid, low = pieces(scaled, 3)
    tiles = [high, mid, high, mid, low, high]
    tiles.append(norm_tile(rows, 3, dist, 1.0))
    tiles.append(norm_tile(rows, 3, size, 1.0))
    return jnp.concatenate(tiles, axis=0).astype(BF16)


def left_features(tile):
    rows, scaled, dist, size = split_state(tile)
    high, mid, low = pieces(2.0 * scaled, 3)
    tiles = [high, high, mid, mid, high, low]
    tiles.append(norm_tile(rows, 0, -dist, -1.0))
    tiles.append(norm_tile(rows, 0, size, 1.0))
    return jnp.concatenate(tiles, axis=0).T.astype(BF16)


def left_pair(features):
    lane = lax.broadcasted_iota(jnp.int32, features.shape, 1)
    to_dist = ((lane < 48) & (lane % 8 != 7)) | ((lane >= 48) & (lane < 56))
    zero = jnp.zeros_like(features)
    return jnp.concatenate(
        [jnp.where(to_dist, zero, features), jnp.where(to_dist, features, zero)], axis=0
    )


def sums(tile):
    rows = row_ids(tile.shape)
    kept = jnp.where(rows < 4, tile * tile[3:4], 0.0)
    high, mid, low = pieces(kept, 3)
    return jnp.concatenate([high, mid, low, jnp.zeros_like(high)], axis=0).astype(BF16)


def weigh(pair, weight):
    size, dist = pair[0:LANES], pair[LANES : 2 * LANES]
    inverse = pl.reciprocal(size, approx=True)
    value = jnp.exp2((dist * inverse) * (2.0 - size * inverse))
    high = value.astype(BF16)
    weight[0] = high
    weight[1] = (value - high.astype(F32)).astype(BF16)


def over_right(summed, weight):
    dims = (((1,), (1,)), ((), ()))
    return lax.dot_general(summed, weight[0], dims, preferred_element_type=F32) + lax.dot_general(
        summed, weight[1], dims, preferred_element_type=F32
    )


def over_left(summed, high, low):
    return jnp.dot(summed, high, preferred_element_type=F32) + jnp.dot(
        summed, low, preferred_element_type=F32
    )


def pull(tile, product):
    total = product[0:8] + product[8:16] + product[16:24]
    return tile[3:4] * (tile * total[3:4] - total)


def local_kernel(state, ahead, force, features, summed, right, pair, weight):
    del ahead
    blocks = features.shape[0]
    force[...] = jnp.zeros(force.shape, F32)
    weight[...] = jnp.zeros(weight.shape, BF16)
    pair[...] = jnp.ones(pair.shape, F32)

    def prepare(b, carry):
        tile = state[b]
        features[b] = left_features(tile)
        right[b] = right_features(tile)
        summed[b] = sums(tile)
        return carry

    lax.fori_loop(0, blocks, prepare, 0, unroll=4)
    right[blocks] = right_features(state[blocks])
    summed[blocks] = sums(state[blocks])

    def turn(i, now):
        live = i >= 2
        ends = []
        for k in range(WIDE):
            done = jnp.maximum(WIDE * (i - 2) + k, 0)
            held = weight.at[now, k]
            on_here = over_right(jnp.concatenate([summed[done], summed[done + 1]], axis=1), held)
            on_beside = over_left(summed[done], held[0, :, LANES:], held[1, :, LANES:])
            ends.append((done, on_here, on_beside))
        for k in range(WIDE):
            weigh(pair.at[1 - now, k], weight.at[1 - now, k])
        for k in range(WIDE):
            b = jnp.minimum(WIDE * i + k, blocks - 1)
            pair[now, k] = jnp.dot(
                left_pair(features[b]),
                jnp.concatenate([right[b], right[b + 1]], axis=1),
                preferred_element_type=F32,
            )
        for done, on_here, on_beside in ends:
            force[done] = force[done] + jnp.where(live, pull(state[done], on_here), 0.0)
            force[done + 1] = force[done + 1] + jnp.where(live, pull(state[done + 1], on_beside), 0.0)

    def step(i, carry):
        turn(2 * i, 0)
        turn(2 * i + 1, 1)
        return carry

    lax.fori_loop(0, (blocks // WIDE + 2) // 2, step, 0)


def label_kernel(came, listed, total, tags, sem):
    slot_total = came.shape[0]
    fetch = pltpu.make_async_copy(came.at[:, 3, :], tags, sem)
    fetch.start()
    fetch.wait()

    def pick(s, count):
        block = tags[s, 0].astype(jnp.int32) - 1
        listed[count, 0] = s
        listed[count, 1] = jnp.maximum(block, 0)
        return count + jnp.where(block >= 0, 1, 0)

    count = lax.fori_loop(0, slot_total, pick, 0, unroll=8)
    spare = lax.axis_index("gx") * CAP
    for extra in range(UNROLL):
        listed[count + extra, 0] = spare
        listed[count + extra, 1] = 0
    total[0] = count


def remote_kernel(
    listed, total, state, features, summed, force_in, came, force, back, right, others, tiles, pair, weight
):
    force[...] = force_in[...]
    weight[...] = jnp.zeros(weight.shape, BF16)
    pair[...] = jnp.ones(pair.shape, F32)
    rows = row_ids((8, LANES))
    tag = (rows == 3) & (lax.broadcasted_iota(jnp.int32, (8, LANES), 1) == 0)
    count = total[0]

    def prepare(i, carry):
        for u in range(UNROLL):
            at = i * UNROLL + u
            raw = came[listed[at, 0]]
            tile = jnp.where(tag, jnp.minimum(raw, 1.0), raw)
            tiles[at] = tile
            right[at] = right_features(tile)
            others[at] = sums(tile)
        return carry

    groups = (count + UNROLL) // UNROLL
    last = UNROLL * groups - 1
    lax.fori_loop(0, groups, prepare, 0)

    def turn(i, now):
        live = i >= 2
        ends = []
        for k in range(WIDE):
            done = jnp.clip(WIDE * (i - 2) + k, 0, last)
            block = listed[done, 1]
            held = weight.at[now, k]
            on_own = over_right(others[done], held)
            on_other = over_left(summed[block], held[0], held[1])
            ends.append((done, block, on_own, on_other))
        for k in range(WIDE):
            weigh(pair.at[1 - now, k], weight.at[1 - now, k])
        for k in range(WIDE):
            at = jnp.minimum(WIDE * i + k, last)
            pair[now, k] = jnp.dot(
                left_pair(features[listed[at, 1]]), right[at], preferred_element_type=F32
            )
        for done, block, on_own, on_other in ends:
            force[block] = force[block] + jnp.where(live, pull(state[block], on_own), 0.0)
            back[listed[done, 0]] = pull(tiles[done], on_other)[0:4]

    def step(i, carry):
        turn(2 * i, 0)
        turn(2 * i + 1, 1)
        return carry

    lax.fori_loop(0, groups + 1, step, 0)


def scatter_kernel(
    cells_dev, owner, cell, vel, rad, speed, slope, after, out, columns, lines, copies, acc, split, left, right
):
    del after
    for g in range(copies.shape[0]):
        for c in range(3):
            copies[g, c] = speed[c]
            copies[g, 3 + c] = slope[c]
    here = cell[...]
    brick = here // cells_dev
    stored = jnp.zeros_like(here)
    for j in range(owner.shape[0]):
        stored = jnp.where(brick == j, owner[j], stored)
    stored = jnp.where(here >= 0, stored * cells_dev + (here & (cells_dev - 1)), 0)
    columns[...] = (stored & 127) + ((stored >> 13) << 7)
    lines[...] = (stored >> 7) & 63
    amount = jnp.where(here >= 0, drag_coeff * rad[...], 0.0)
    for c in range(4):
        high, low = pieces(amount if c == 0 else amount * vel[c - 1], 2)
        split[2 * c] = high
        split[2 * c + 1] = low
    acc[...] = jnp.zeros(acc.shape, F32)
    chunk = left.shape[2] // LANES
    chunks = cell.shape[0] // chunk

    def build(t, buf):
        fine = row_ids((SPLIT, LANES))
        coarse = row_ids((64, LANES))
        for u in range(chunk):
            at = pl.ds(t * chunk + u, 1)
            lo = u * LANES
            right[buf, :, lo : lo + LANES] = jnp.where(fine == columns[at, :], 1.0, 0.0).astype(BF16)
            mask = coarse == lines[at, :]
            for p in range(8):
                left[buf, 64 * p : 64 * p + 64, lo : lo + LANES] = jnp.where(
                    mask, split[p, at, :], 0.0
                ).astype(BF16)

    build(0, 0)

    def step(i, carry):
        for now in range(2):
            t = 2 * i + now
            acc[...] += lax.dot_general(
                left[now], right[now], (((1,), (1,)), ((), ())), preferred_element_type=F32
            )
            build(jnp.minimum(t + 1, chunks - 1), 1 - now)
        return carry

    lax.fori_loop(0, chunks // 2, step, 0)
    for g in range(out.shape[0]):
        for c in range(4):
            lo = (g // 4) * LANES
            at = c * 128 + (g % 4) * 16
            out[g, c] = acc[at : at + 16, lo : lo + LANES] + acc[at + 64 : at + 80, lo : lo + LANES]


def gather_kernel(columns, lines, cell, vel, rad, table, parts, speed, fluid, out, wide, picked, found):
    whole = [sum(parts[g, c] for g in range(parts.shape[0])) for c in range(4)]
    for c in range(3):
        out[c] = whole[1 + c] - speed[c] * whole[0]
    for owner in range(table.shape[0]):
        high, low = pieces(table[owner].reshape(96, LANES), 2)
        wide[0, owner // 4, owner % 4] = high.astype(BF16)
        wide[1, owner // 4, owner % 4] = low.astype(BF16)
    chunks = cell.shape[0] // 2

    def look(t, buf):
        fine = row_ids((SPLIT, LANES))
        hot = jnp.concatenate(
            [
                jnp.where(fine == columns[pl.ds(2 * t + u, 1), :], 1.0, 0.0).astype(BF16)
                for u in range(2)
            ],
            axis=1,
        )
        total = None
        for p in range(2):
            side = jnp.concatenate([wide[p, half].reshape(384, LANES) for half in range(2)], axis=1)
            term = jnp.dot(side, hot, preferred_element_type=F32)
            total = term if total is None else total + term
        picked[buf] = total

    look(0, 0)

    def step(i, carry):
        for now in range(2):
            t = 2 * i + now
            coarse = row_ids((64, LANES))
            for u in range(2):
                at = pl.ds(2 * t + u, 1)
                lo = u * LANES
                mask = coarse == lines[at, :]
                for c in range(6):
                    total = None
                    for q in range(4):
                        row = q * 96 + c * 16
                        term = jnp.where(
                            mask[q * 16 : q * 16 + 16], picked[now, row : row + 16, lo : lo + LANES], 0.0
                        )
                        total = term if total is None else total + term
                    found[c, at, :] = jnp.sum(total, axis=0, keepdims=True)
            look(jnp.minimum(t + 1, chunks - 1), 1 - now)
        return carry

    lax.fori_loop(0, chunks // 2, step, 0)
    size = rad[...]
    live = (cell[...] >= 0).astype(F32)
    cube = size * size * size
    for c in range(3):
        drag = live * drag_coeff * size * (found[c] - vel[c])
        fluid[c] = drag - live * cube * found[3 + c]


def final_kernel(slots, mine, force, back, fluid, vel, rad, out, total):
    blocks = rad.shape[0]
    total[...] = force[0:blocks]

    def add(p, carry):
        block = mine[p]
        total[block, 0:4] = total[block, 0:4] + back[slots[p]]
        return carry

    lax.fori_loop(0, mine.shape[0], add, 0, unroll=4)
    size = rad[...]
    cube = size * size * size
    for c in range(3):
        out[c] = vel[c] + time_step * (total[:, c, :] + fluid[c]) / cube


def call(body, outs, args, smem=(), smem_out=(), raw=(), raw_out=(), scratch=(), alias=None, flops=0):
    return pl.pallas_call(
        body,
        out_shape=[jax.ShapeDtypeStruct(s, d) for s, d in outs],
        in_specs=[SMEM_SPEC if i in smem else RAW_SPEC if i in raw else VMEM_SPEC for i in range(len(args))],
        out_specs=[
            SMEM_SPEC if i in smem_out else RAW_SPEC if i in raw_out else VMEM_SPEC
            for i in range(len(outs))
        ],
        scratch_shapes=list(scratch),
        input_output_aliases=alias or {},
        cost_estimate=pl.CostEstimate(flops=flops, bytes_accessed=1 << 20, transcendentals=0),
    )(*args)


def on_device(
    positions,
    velocities,
    radius,
    sphere_cell,
    pair_route,
    pair_mine,
    pair_theirs,
    brick_owner,
    fluid_velocity,
    pressure_grad,
):
    gx_count, gy_count = lax.axis_size("gx"), lax.axis_size("gy")
    blocks = positions.shape[2] // LANES
    cells_dev = fluid_velocity.shape[2]
    cell_rows = cells_dev // LANES
    pairs = pair_mine.shape[1]
    slot_total = gx_count * CAP
    pos = positions.reshape(3, blocks, LANES)
    vel = velocities.reshape(3, blocks, LANES)
    rad = radius.reshape(blocks, LANES)
    cell = sphere_cell.reshape(blocks, LANES)
    speed = fluid_velocity.reshape(3, cell_rows, LANES)
    slope = pressure_grad.reshape(3, cell_rows, LANES)
    route, mine, theirs = pair_route.reshape(pairs), pair_mine.reshape(pairs), pair_theirs.reshape(pairs)

    push, slots, state = call(
        functools.partial(prep_kernel, gx_count),
        [((slot_total, 8, LANES), F32), ((pairs,), jnp.int32), ((blocks + 1, 8, LANES), F32)],
        (route, mine, theirs, pos, vel, rad, cell),
        smem=(0, 1, 2),
        smem_out=(1,),
        scratch=[pltpu.SMEM((gx_count,), jnp.int32)],
    )
    came = exchange(push.reshape(gx_count, CAP * 8, LANES), "gx")
    came = came.reshape(slot_total, 8, LANES)

    parts, columns, lines, copies = call(
        functools.partial(scatter_kernel, cells_dev),
        [
            ((gy_count, 4, cell_rows, LANES), F32),
            ((blocks, LANES), jnp.int32),
            ((blocks, LANES), jnp.int32),
            ((gy_count, 6, cell_rows, LANES), F32),
        ],
        (brick_owner.reshape(-1), cell, vel, rad, speed, slope, slots),
        smem=(0, 6),
        scratch=[
            pltpu.VMEM((512, SPLIT), F32),
            pltpu.VMEM((8, blocks, LANES), F32),
            pltpu.VMEM((2, 512, CHUNK * LANES), BF16),
            pltpu.VMEM((2, SPLIT, CHUNK * LANES), BF16),
        ],
        flops=2 * 10**9,
    )
    listed, total = call(
        label_kernel,
        [((slot_total + UNROLL, 2), jnp.int32), ((1,), jnp.int32)],
        (came,),
        smem_out=(0, 1),
        raw=(0,),
        scratch=[pltpu.SMEM((slot_total, LANES), F32), pltpu.SemaphoreType.DMA],
    )
    force, features, summed = call(
        local_kernel,
        [
            ((blocks + 1, 8, LANES), F32),
            ((blocks, LANES, 64), BF16),
            ((blocks + 1, 32, LANES), BF16),
        ],
        (state, total),
        flops=4 * 10**9,
        raw=(1,),
        scratch=[
            pltpu.VMEM((blocks + 1, 64, LANES), BF16),
            pltpu.VMEM((2, WIDE, 2 * LANES, 2 * LANES), F32),
            pltpu.VMEM((2, WIDE, 2, LANES, 2 * LANES), BF16),
        ],
    )
    table = exchange(copies.reshape(gy_count, 6 * cell_rows, LANES), "gy")
    table = table.reshape(gy_count, 6, cell_rows, LANES)
    parts = exchange(parts.reshape(gy_count, 4 * cell_rows, LANES), "gy")
    parts = parts.reshape(gy_count, 4, cell_rows, LANES)

    room = slot_total + UNROLL
    force, back = call(
        remote_kernel,
        [((blocks + 1, 8, LANES), F32), ((slot_total, 4, LANES), F32)],
        (listed, total, state, features, summed, force, came),
        smem=(0, 1),
        scratch=[
            pltpu.VMEM((room, 64, LANES), BF16),
            pltpu.VMEM((room, 32, LANES), BF16),
            pltpu.VMEM((room, 8, LANES), F32),
            pltpu.VMEM((2, WIDE, 2 * LANES, LANES), F32),
            pltpu.VMEM((2, WIDE, 2, LANES, LANES), BF16),
        ],
        alias={5: 0},
        flops=4 * 10**9,
    )
    back = exchange(back.reshape(gx_count, CAP * 4, LANES), "gx")
    back = back.reshape(slot_total, 4, LANES)

    fluid, drag_source = call(
        gather_kernel,
        [((3, blocks, LANES), F32), ((3, cell_rows, LANES), F32)],
        (columns, lines, cell, vel, rad, table, parts, speed),
        scratch=[
            pltpu.VMEM((2, 2, 4, 96, LANES), BF16),
            pltpu.VMEM((2, 384, 2 * LANES), F32),
            pltpu.VMEM((6, blocks, LANES), F32),
        ],
        flops=3 * 10**9,
    )
    (new_velocity,) = call(
        final_kernel,
        [((3, blocks, LANES), F32)],
        (slots, mine, force, back, fluid, vel, rad),
        smem=(0, 1),
        scratch=[pltpu.VMEM((blocks, 8, LANES), F32)],
    )
    return new_velocity.reshape(3, 1, blocks * LANES), drag_source.reshape(3, 1, cells_dev)


def exchange(value, axis):
    return lax.all_to_all(value, axis, 0, 0, tiled=True)


def solution(mesh):
    placed = (
        P(None, "gx", "gy"),
        P(None, "gx", "gy"),
        P("gx", "gy"),
        P("gx", "gy"),
        P("gx", "gy", None),
        P("gx", "gy"),
        P("gx", "gy"),
        P("gx", None),
        P(None, "gx", "gy"),
        P(None, "gx", "gy"),
    )
    return jax.shard_map(
        on_device,
        mesh=mesh,
        in_specs=placed,
        out_specs=(P(None, "gx", "gy"), P(None, "gx", "gy")),
        check_vma=False,
    )
```

time: 488 us -> 89.2 us (0.18)
  blocking collectives: 205 us -> 0 us
  other arithmetic: 149 us -> 0 us
  local copies, waits for them, and re-layouts: 83.3 us -> 0.7 us
  Pallas kernels: 0 us -> 49.5 us
  between operations: 14.4 us -> 0.69 us
    all_gather x2 -> x0, blocking collectives: 205 us -> none  [the longest x1 118 us: on_device(): lax.all_gather(pressure_grad, 'gy', axis=2, tiled=True)]
    gather x4 -> x0, local copies, waits for them, and re-layouts: 63.7 us -> none  [the longest x1 31.1 us: on_device(): grad_at = jnp.take(column_p[:, 0], storage, axis=1)]
    scatter-add x1 -> x0, other arithmetic: 56 us -> none  [on_device(): jax.ops.segment_sum(-drag_force.T, storage, num_segments=gy_count * cells...]
    reduce_sum x34 -> x0, other arithmetic: 50.7 us -> none  [the longest x32 49.8 us: contact(): return (jnp.sum(pulling, axis=3), -jnp.sum(pulling, axis=2))]
    pallas_call x0 -> x7, Pallas kernels: none -> 49.5 us  [call(): pl.pallas_call(body, out_shape=[jax.ShapeDtypeStruct(s, d) for s, d in ou...]
    sub x32 -> x0, other arithmetic: 14.9 us -> none  [contact(): offset = left_state[:, 0:3, :, None] - right_state[:, 0:3, None, :]]
    mul x35 -> x0, other arithmetic: 12.5 us -> none  [the longest x32 11.5 us: contact(): pulling = weight[:, None] * (stiffness * offset - damping * relative)]
    reshape x1 -> x0, other arithmetic: 10.1 us -> none  [on_device(): return (new_velocity.reshape(3, 1, sphere_total), drag_source)]
  transfers between devices with their start and end apart: 4 -> 4, of which waited for: 1 -> 3; matrix products, arithmetic and copies ran while one was open for 35% -> 0% of each run, Pallas kernels for 0% -> 51%
where the time goes in v1:
time: 89.2 us; the launch traced here: 88.5 us
  Pallas kernels  49.5 us (55%)
  starting transfers between devices  25.7 us (29%)
  waiting for transfers between devices  11.9 us (13%)
    pallas_call x7, Pallas kernels, call(): pl.pallas_call(body, out_shape=[jax.ShapeDtypeStruct(s, d) for s, d in ou...  49.5 us
    all_to_all x4, starting transfers between devices, exchange(): return lax.all_to_all(value, axis, 0, 0, tiled=True)  25.7 us
    all_to_all x4, waiting for transfers between devices, exchange(): return lax.all_to_all(value, axis, 0, 0, tiled=True)  11.9 us
  transfers between devices with their start and end apart: 4, of which 3 were waited for; matrix products, arithmetic and copies ran while one was open for 0% of the time, Pallas kernels for 51%

profile of v1, /device:TPU:1, one launch (start us, length us, event | category | flops | bytes accessed | tf_op | source)
XLA Modules:
  0.0 88.5 jit_solution(254139599724447446)
XLA Ops:
  0.6 2.6 %shard_map.113 = (f32[128,8,128]{2,1,0:T(8,128)}, s32[64]{0:T(128)}, f32[65,8,128]{2,1,0:T(8,128)}) custom-call(s32[64]{0:T(128)} %bitcast.44, s32[64]{0:T(128)} %bitcast.42, s32[64]{0:T(128)} %bitcast.45, f32[3,64,128]{2,1,0:T(8,128)} %bitcast.37, f32[3,64,128]{2,1,0:T(8,128)} %bitcast.26, f32[64,128]{1,0:T(8,128)} %bitcast.33, s32[64,128]{1,0:T(8,128)} %bitcast.39), custom_call_target="tpu_custom_call" | custom-call | bytes 1048576 | tf_op jit(solution)/shard_map/pallas_call | solution.py:406
  3.2 8.6 %all-to-all-start = ((f32[32,32,128]{2,1,0:T(8,128)}), f32[32,32,128]{2,1,0:T(8,128)S(1)}, u32[]{:S(2)}, u32[]{:S(2)}) async-start(f32[32,32,128]{2,1,0:T(8,128)} %bitcast.23), calls=%async_computation | async-start | bytes 1048576 | tf_op jit(solution)/shard_map/all_to_all | solution.py:545
  11.8 6.6 %shard_map.117 = (f32[8,4,16,128]{3,2,1,0:T(8,128)}, s32[64,128]{1,0:T(8,128)}, s32[64,128]{1,0:T(8,128)}, f32[8,6,16,128]{3,2,1,0:T(8,128)}) custom-call(s32[8]{0:T(128)} %bitcast.49, s32[64,128]{1,0:T(8,128)} %bitcast.40, f32[3,64,128]{2,1,0:T(8,128)} %bitcast.27, f32[64,128]{1,0:T(8,128)} %bitcast.34, f32[3,16,128]{2,1,0:T(8,128)} %bitcast.47, ...), custom_call_target="tpu_custom_call" | custom-call | flops 2000000000 | bytes 1048576 | tf_op jit(solution)/shard_map/pallas_call | solution.py:406
  18.5 4.8 %all-to-all-done = f32[32,32,128]{2,1,0:T(8,128)S(1)} async-done(((f32[32,32,128]{2,1,0:T(8,128)}), f32[32,32,128]{2,1,0:T(8,128)S(1)}, u32[]{:S(2)}, u32[]{:S(2)}) %all-to-all-start) | async-done | bytes 524320 | tf_op jit(solution)/shard_map/all_to_all | solution.py:545
  23.2 0.0 copy-start
  23.2 8.2 %all-to-all-start.3 = ((f32[8,64,128]{2,1,0:T(8,128)}), f32[8,64,128]{2,1,0:T(8,128)S(1)}, u32[]{:S(2)}, u32[]{:S(2)}) async-start(f32[8,64,128]{2,1,0:T(8,128)} %bitcast.32), calls=%async_computation.3 | async-start | bytes 524288 | tf_op jit(solution)/shard_map/all_to_all | solution.py:545
  31.4 0.0 copy-done
  31.4 4.2 %shard_map.114 = (s32[132,2]{1,0:T(8,128)}, s32[1]{0:T(128)}) custom-call(f32[128,8,128]{2,1,0:T(8,128)} %bitcast.20), custom_call_target="tpu_custom_call" | custom-call | bytes 1048576 | tf_op jit(solution)/shard_map/pallas_call | solution.py:406
  35.6 6.8 %all-to-all-done.3 = f32[8,64,128]{2,1,0:T(8,128)S(1)} async-done(((f32[8,64,128]{2,1,0:T(8,128)}), f32[8,64,128]{2,1,0:T(8,128)S(1)}, u32[]{:S(2)}, u32[]{:S(2)}) %all-to-all-start.3) | async-done | bytes 262176 | tf_op jit(solution)/shard_map/all_to_all | solution.py:545
  42.5 0.0 copy-start.3
  42.5 3.5 %all-to-all-start.2 = ((f32[8,96,128]{2,1,0:T(8,128)}), f32[8,96,128]{2,1,0:T(8,128)S(1)}, u32[]{:S(2)}, u32[]{:S(2)}) async-start(f32[8,96,128]{2,1,0:T(8,128)} %bitcast.24), calls=%async_computation.2 | async-start | bytes 786432 | tf_op jit(solution)/shard_map/all_to_all | solution.py:545
  45.9 13.8 %shard_map.115 = (f32[65,8,128]{2,1,0:T(8,128)}, bf16[64,128,64]{2,1,0:T(8,128)(2,1)}, bf16[65,32,128]{2,1,0:T(8,128)(2,1)}) custom-call(f32[65,8,128]{2,1,0:T(8,128)} %get-tuple-element.22.state, s32[1]{0:T(128)} %get-tuple-element.21.ahead.total), custom_call_target="tpu_custom_call" | custom-call | flops 4000000000 | bytes 1048576 | tf_op jit(solution)/shard_map/pallas_call | solution.py:406
  59.7 0.0 copy-done.3
  59.7 11.6 %shard_map.116 = (f32[65,8,128]{2,1,0:T(8,128)}, f32[128,4,128]{2,1,0:T(4,128)}) custom-call(s32[132,2]{1,0:T(8,128)} %get-tuple-element.20.listed, s32[1]{0:T(128)} %get-tuple-element.21.ahead.total, f32[65,8,128]{2,1,0:T(8,128)} %get-tuple-element.22.state, bf16[64,128,64]{2,1,0:T(8,128)(2,1)} %get-tuple-element.23.features, ...), custom_call_target="tpu_custom_call", output_to_operand_aliasing={{0}: (5, {})} | custom-call | flops 4000000000 | bytes 1048576 | tf_op jit(solution)/shard_map/pallas_call | solution.py:406
  71.3 0.0 all-to-all-done.2
  71.3 0.0 copy-start.2
  71.3 5.5 %all-to-all-start.1 = ((f32[32,16,128]{2,1,0:T(8,128)}), f32[32,16,128]{2,1,0:T(8,128)S(1)}, u32[]{:S(2)}, u32[]{:S(2)}) async-start(f32[32,16,128]{2,1,0:T(8,128)} %bitcast.31), calls=%async_computation.1 | async-start | bytes 524288 | tf_op jit(solution)/shard_map/all_to_all | solution.py:545
  76.8 0.0 copy-done.2
  76.8 8.6 %shard_map.118 = (f32[3,64,128]{2,1,0:T(8,128)}, f32[3,16,128]{2,1,0:T(8,128)}) custom-call(s32[64,128]{1,0:T(8,128)} %get-tuple-element.28.columns, s32[64,128]{1,0:T(8,128)} %get-tuple-element.29.lines, s32[64,128]{1,0:T(8,128)} %bitcast.41, f32[3,64,128]{2,1,0:T(8,128)} %bitcast.28, f32[64,128]{1,0:T(8,128)} %bitcast.35, f32[8,6,16,128]{3,2,1,0:T(8,128)} %bitcast.25, ...), custom_call_target="tpu_custom_call" | custom-call | flops 3000000000 | bytes 1048576 | tf_op jit(solution)/shard_map/pallas_call | solution.py:406
  85.4 0.3 all-to-all-done.1
  85.7 0.0 copy-start.1
  85.7 0.7 copy-done.1
  86.4 2.1 %shard_map.119 = f32[3,64,128]{2,1,0:T(8,128)} custom-call(s32[64]{0:T(128)} %get-tuple-element.18.after.slots, s32[64]{0:T(128)} %bitcast.43, f32[65,8,128]{2,1,0:T(8,128)} %get-tuple-element.26.force, f32[128,4,128]{2,1,0:T(4,128)} %bitcast.22, f32[3,64,128]{2,1,0:T(8,128)} %get-tuple-element.32.fluid, f32[3,64,128]{2,1,0:T(8,128)} %bitcast.29, ...), custom_call_target="tpu_custom_call" | custom-call | bytes 1048576 | tf_op jit(solution)/shard_map/pallas_call | solution.py:406
Async XLA Ops:
  3.2 20.0 %all-to-all-start = ((f32[32,32,128]{2,1,0:T(8,128)}), f32[32,32,128]{2,1,0:T(8,128)S(1)}, u32[]{:S(2)}, u32[]{:S(2)}) async-start(f32[32,32,128]{2,1,0:T(8,128)} %bitcast.23), calls=%async_computation | async-start | bytes 1048576 | tf_op jit(solution)/shard_map/all_to_all | solution.py:545
  23.2 8.2 %copy-start = (f32[32,32,128]{2,1,0:T(8,128)}, f32[32,32,128]{2,1,0:T(8,128)S(1)}, u32[]{:S(2)}) copy-start(f32[32,32,128]{2,1,0:T(8,128)S(1)} %all-to-all-done) | copy-start | bytes 1572868
  23.2 19.2 %all-to-all-start.3 = ((f32[8,64,128]{2,1,0:T(8,128)}), f32[8,64,128]{2,1,0:T(8,128)S(1)}, u32[]{:S(2)}, u32[]{:S(2)}) async-start(f32[8,64,128]{2,1,0:T(8,128)} %bitcast.32), calls=%async_computation.3 | async-start | bytes 524288 | tf_op jit(solution)/shard_map/all_to_all | solution.py:545
  42.5 17.3 %copy-start.3 = (f32[8,64,128]{2,1,0:T(8,128)}, f32[8,64,128]{2,1,0:T(8,128)S(1)}, u32[]{:S(2)}) copy-start(f32[8,64,128]{2,1,0:T(8,128)S(1)} %all-to-all-done.3) | copy-start | bytes 786436
  42.5 28.9 %all-to-all-start.2 = ((f32[8,96,128]{2,1,0:T(8,128)}), f32[8,96,128]{2,1,0:T(8,128)S(1)}, u32[]{:S(2)}, u32[]{:S(2)}) async-start(f32[8,96,128]{2,1,0:T(8,128)} %bitcast.24), calls=%async_computation.2 | async-start | bytes 786432 | tf_op jit(solution)/shard_map/all_to_all | solution.py:545
  71.3 5.5 %copy-start.2 = (f32[8,96,128]{2,1,0:T(8,128)}, f32[8,96,128]{2,1,0:T(8,128)S(1)}, u32[]{:S(2)}) copy-start(f32[8,96,128]{2,1,0:T(8,128)S(1)} %all-to-all-done.2) | copy-start | bytes 1179652
  71.3 14.4 %all-to-all-start.1 = ((f32[32,16,128]{2,1,0:T(8,128)}), f32[32,16,128]{2,1,0:T(8,128)S(1)}, u32[]{:S(2)}, u32[]{:S(2)}) async-start(f32[32,16,128]{2,1,0:T(8,128)} %bitcast.31), calls=%async_computation.1 | async-start | bytes 524288 | tf_op jit(solution)/shard_map/all_to_all | solution.py:545
  85.7 0.7 copy-start.1
